TPU v7x, 32 devices: a whole 2x2x4 slice. The times are simulated.
32 devices in a mesh: psg: 8 (over z, x), mp: 4 (over y, core).
Axes of the slice: x: 2, y: 2, z: 4, core: 2. Of those that a mesh axis runs over, the one named last changes fastest.
Arguments:
- tokens: bfloat16 [8192, 4096], P('psg'), may hold values from -6 to 6
- lengths: int32 [32], P('psg'), may hold values from 32 to 256, as said below
- assignment: int32 [32], P('psg'), may hold values from 0 to 3, as said below
- retrieval: float32 [32], P('psg'), may hold values from -8 to 306
- enc_gain: float32 [4096], replicated, may hold values from 0.25 to 1.75
- enc_qkv: bfloat16 [3, 4096, 2048], P(None, 'psg', 'mp'), may hold values from -0.09375 to 0.09375
- position_bias: float32 [32, 32], P('mp'), may hold values from -6 to 306
- enc_output: bfloat16 [2048, 4096], P('mp', 'psg'), may hold values from -0.125 to 0.125
- final_gain: float32 [4096], replicated, may hold values from 0.25 to 1.75
- embedding: bfloat16 [32128, 4096], P('mp', 'psg'), may hold values from -18 to 18
- dec_tokens: int32 [4, 2], replicated, may hold values from 0 to 32127
- dec_gain: float32 [4096], P('psg'), may hold values from 0.25 to 1.75
- cross_query: bfloat16 [4096, 2048], P('psg', 'mp'), may hold values from -0.0234375 to 0.0234375
- cross_keyval: bfloat16 [2, 4096, 2048], P(None, 'psg', 'mp'), may hold values from -0.09375 to 0.09375
- cross_output: bfloat16 [2048, 4096], P('mp', 'psg'), may hold values from -0.25 to 0.25
Outputs:
- encoded: bfloat16 [8192, 4096], P('psg', 'mp')
- decoded: bfloat16 [4, 2, 4096], P(None, None, ('psg', 'mp'))
Inputs may be any that keep to these rules, and one draw needn't show every extreme that they name: Passage p holds real tokens in its first lengths[p] slots and padding after them; in every draw all passages of some index of psg have 256 real tokens. `assignment`: every claim has exactly 8 passages.
All inputs are finite; a program needn't handle non-finite values.
Results may differ from a plain program's by a relative error of at most 0.013.
The roundings to bfloat16 on the way count: a program that leaves them out, or rounds other values in their place, can miss the bound.
Values may be sent and summed in bfloat16 or wider, within the bound.
No kernel may reach another device: no remote copies, remote signals or barrier semaphores. Data moves between devices by JAX's collectives and lax.ppermute only.
A program may use at most 128 MiB of HBM per device.

v0:
```python
import math
import jax
import jax.numpy as jnp
import numpy as np
from jax import lax
from jax.sharding import PartitionSpec as P

D = 4096
HEAD_DIM = 64
BUCKETS = 32
MAXDIST = 128
SEQ = 256
CLAIMS = 4
POS = 2
EPSILON = 1e-06
MASKED = -1e30
HIGHEST = lax.Precision.HIGHEST


def merged(value, axis, combine):
    everything = jax.tree.map(lambda part: lax.all_gather(part, axis), value)
    first = jax.tree.map(lambda part: part[0], everything)

    def turn(k, so_far):
        return combine(so_far, jax.tree.map(lambda part: part[k], everything))

    return lax.fori_loop(1, lax.axis_size(axis), turn, first)


def bucket_onehot(length, buckets, max_distance):
    halfway = buckets // 2
    exact_max = halfway // 2
    relative_list = list(range(-(length - 1), length))
    beyond_list = [
        min(
            halfway - 1,
            exact_max
            + math.floor(
                math.log(max(abs(shift), 1) / exact_max)
                / math.log(max_distance / exact_max)
                * (halfway - exact_max)
            ),
        )
        for shift in relative_list
    ]
    relative = np.array(relative_list)
    beyond = np.array(beyond_list)
    distance = np.abs(relative)
    bucket_ids = np.where(relative > 0, halfway, 0) + np.where(
        distance < exact_max, distance, beyond
    )
    return (bucket_ids[None, :] == np.arange(buckets)[:, None]).astype(np.float32)


def toeplitz(vectors):
    heads_count, width_all = vectors.shape
    length = (width_all + 1) // 2
    padded = jnp.concatenate([vectors, jnp.zeros((heads_count, 1), vectors.dtype)], axis=1)
    rolled = jnp.roll(padded, -(length - 1), axis=1)
    repeated = jnp.tile(rolled, (1, length))[:, : length * (2 * length - 1)]
    return repeated.reshape(heads_count, length, 2 * length - 1)[:, :, :length]


def rms_norm(values, norm_gain):
    values = values.astype(jnp.float32)
    inverse = lax.rsqrt(jnp.mean(values * values, axis=-1, keepdims=True) + EPSILON)
    return values * inverse * norm_gain


def combine_partial(first, second):
    first_max, first_total, first_acc = first
    second_max, second_total, second_acc = second
    joint_max = jnp.maximum(first_max, second_max)
    first_scale = jnp.exp(first_max - joint_max)
    second_scale = jnp.exp(second_max - joint_max)
    joint_total = first_total * first_scale + second_total * second_scale
    joint_acc = first_acc * first_scale[..., None] + second_acc * second_scale[..., None]
    return (joint_max, joint_total, joint_acc)


def shards(
    tokens,
    lengths,
    assignment,
    retrieval,
    enc_gain,
    enc_qkv,
    position_bias,
    enc_output,
    final_gain,
    embedding,
    dec_tokens,
    dec_gain,
    cross_query,
    cross_keyval,
    cross_output,
):
    tok_rows = tokens.shape[0]
    model_width = tokens.shape[1]
    passages_here = lengths.shape[0]
    width_here = enc_qkv.shape[1]
    inner_here = enc_qkv.shape[2]
    heads_here = inner_here // HEAD_DIM
    query_rows = CLAIMS * POS
    positions = jnp.arange(SEQ)
    groups_count = lax.axis_size("mp")
    normed = rms_norm(tokens, enc_gain).astype(jnp.bfloat16)
    projected = jnp.einsum(
        "td,kdc->ktc",
        normed,
        lax.all_gather(enc_qkv, "psg", axis=1, tiled=True),
        preferred_element_type=jnp.float32,
    )
    shaped = projected.astype(jnp.bfloat16).reshape(3, passages_here, SEQ, heads_here, HEAD_DIM)
    bias_table = jnp.dot(
        position_bias, jnp.asarray(bucket_onehot(SEQ, BUCKETS, MAXDIST)), precision=HIGHEST
    )
    pair_bias = toeplitz(bias_table)
    scores = (
        jnp.einsum("pihd,pjhd->phij", shaped[0], shaped[1], preferred_element_type=jnp.float32)
        + pair_bias[None]
    )
    valid_keys = positions[None, :] < lengths[:, None]
    scores = jnp.where(valid_keys[:, None, None, :], scores, MASKED)
    weights = jnp.exp(scores - jnp.max(scores, axis=-1, keepdims=True))
    probabilities = (weights / jnp.sum(weights, axis=-1, keepdims=True)).astype(jnp.bfloat16)
    attended = jnp.einsum(
        "phij,pjhd->pihd", probabilities, shaped[2], preferred_element_type=jnp.float32
    )
    attended = attended.astype(jnp.bfloat16).reshape(tok_rows, inner_here)
    share_width = model_width // groups_count
    share_start = lax.axis_index("mp") * share_width
    partial_out = jnp.dot(
        attended,
        lax.all_gather(enc_output, "psg", axis=1, tiled=True),
        preferred_element_type=jnp.float32,
    ).astype(jnp.bfloat16)
    summed = lax.psum(partial_out, "mp").astype(jnp.float32)
    encoded_full = (tokens.astype(jnp.float32) + summed).astype(jnp.bfloat16)
    encoded = lax.dynamic_slice_in_dim(encoded_full, share_start, share_width, 1)
    memory = rms_norm(encoded_full, final_gain).astype(jnp.bfloat16)
    vocab_here = embedding.shape[0]
    token_ids = dec_tokens.reshape(-1) - lax.axis_index("mp") * vocab_here
    lookup = (token_ids[:, None] == jnp.arange(vocab_here)[None, :]).astype(jnp.bfloat16)
    found_rows = jnp.dot(lookup, embedding, preferred_element_type=jnp.float32).astype(jnp.bfloat16)
    embedded = lax.psum(found_rows, "mp").astype(jnp.float32)
    query_weight = cross_query.astype(jnp.float32)
    squares_dec = lax.psum(jnp.sum(embedded * embedded, axis=1), "psg")
    dquery = embedded * lax.rsqrt(squares_dec / D + EPSILON)[:, None] * dec_gain
    cquery = lax.psum(jnp.dot(dquery, query_weight, precision=HIGHEST), "psg")
    cquery = cquery.reshape(query_rows, heads_here, HEAD_DIM)
    row_claim = jnp.arange(query_rows) // POS
    usable = (row_claim[:, None, None] == assignment[None, :, None]) & (
        positions[None, None, :] < lengths[None, :, None]
    )
    usable = usable.reshape(query_rows, 1, tok_rows)
    key_bias = jnp.broadcast_to(retrieval[:, None], (passages_here, SEQ)).reshape(tok_rows)
    key_weight = cross_keyval[0].astype(jnp.float32).reshape(width_here, heads_here, HEAD_DIM)
    folded = jnp.einsum("rhj,dhj->rhd", cquery, key_weight, precision=HIGHEST)
    folded_all = lax.all_gather(folded.astype(jnp.bfloat16), "psg", axis=2, tiled=True).astype(
        folded.dtype
    )
    memory_wide = memory.astype(jnp.float32)
    cross_scores = jnp.einsum("td,rhd->rht", memory_wide, folded_all, precision=HIGHEST) + key_bias
    masked = jnp.where(usable, cross_scores, MASKED)
    local_max = jnp.max(masked, axis=-1)
    weights_c = jnp.where(usable, jnp.exp(masked - local_max[..., None]), 0.0)
    local_max, weights_c = (local_max, weights_c)
    local_total = jnp.sum(weights_c, axis=-1)
    pooled = jnp.einsum("rht,td->rhd", weights_c, memory_wide, precision=HIGHEST)
    joint_max, joint_total, joint_pool = merged(
        (local_max, local_total, pooled), "psg", combine_partial
    )
    own_pool = (
        lax.dynamic_slice_in_dim(joint_pool, lax.axis_index("psg") * width_here, width_here, 2)
        / joint_total[..., None]
    )
    value_weight = cross_keyval[1].astype(jnp.float32).reshape(width_here, heads_here, HEAD_DIM)
    value_terms = jnp.einsum("rhd,dhj->rhj", own_pool, value_weight, precision=HIGHEST)
    cross_attn = lax.psum(value_terms, "psg")
    out_part = jnp.dot(
        cross_attn.reshape(query_rows, inner_here),
        cross_output.astype(jnp.float32),
        precision=HIGHEST,
    )
    out_share = lax.psum_scatter(out_part, "mp", scatter_dimension=1, tiled=True)
    piece_width = out_share.shape[1]
    residual = lax.dynamic_slice_in_dim(
        embedded, lax.axis_index("mp") * piece_width, piece_width, 1
    )
    decoded = (residual + out_share).astype(jnp.bfloat16).reshape(CLAIMS, POS, piece_width)
    return (encoded, decoded)


def solution(mesh):
    in_specs = (
        P("psg", None),
        P("psg"),
        P("psg"),
        P("psg"),
        P(),
        P(None, "psg", "mp"),
        P("mp", None),
        P("mp", "psg"),
        P(),
        P("mp", "psg"),
        P(),
        P("psg"),
        P("psg", "mp"),
        P(None, "psg", "mp"),
        P("mp", "psg"),
    )
    out_specs = (P("psg", "mp"), P(None, None, ("psg", "mp")))
    return jax.shard_map(shards, mesh=mesh, in_specs=in_specs, out_specs=out_specs, check_vma=False)
```

profile of v0, /device:TPU:0, one launch (start us, length us, event | category | flops | bytes accessed | tf_op | source)
XLA Modules:
  0.0 641.4 jit_solution(5036497669544402802)
XLA Ops:
  7.2 0.7 all-gather.7.cloned.1.call-update
  8.0 0.7 all-gather.9.cloned.1.call-update
  8.7 1.0 convolution_bitcast_fusion.1
  9.9 0.5 tile.4
  10.4 2.2 slice.61
  12.6 7.9 %reshape.172 = f32[8,256,511]{2,1,0:T(8,128)} reshape(f32[8,130816]{1,0:T(8,128)} %slice.61) | data formatting | bytes 8372224 | tf_op jit(solution)/shard_map/reshape | solution.py:61
  20.5 2.2 slice.62
  22.7 2.1 copy.44
  24.9 5.1 fusion.7
  29.9 159.1 %all-gather.7.cloned.1.call-done = bf16[3,4096,512]{2,1,0:T(8,128)(2,1)} async-done(((bf16[3,512,512]{2,1,0:T(8,128)(2,1)}), bf16[3,4096,512]{2,1,0:T(8,128)(2,1)}) %all-gather.7.cloned.1.call-update) | async-done | bytes 12582928 | tf_op jit(solution)/shard_map/all_gather | solution.py:111
  189.0 18.3 %convert_bitcast_fusion = bf16[3,1024,512]{2,1,0:T(8,128)(2,1)S(1)} fusion(bf16[3,4096,512]{2,1,0:T(8,128)(2,1)} %all-gather.7.cloned.1.call-done, bf16[1024,4096]{1,0:T(8,128)(2,1)} %param.18, f32[4096]{0:T(1024)S(1)} %copy-done.10, f32[1024]{0:T(1024)S(1)} %add_rsqrt_fusion.1), kind=kOutput, calls=%fused_computation.37 | convolution fusion | flops 12903251968 | bytes 24137728 | tf_op jit(solution)/shard_map/td,kdc->ktc/dot_general | solution.py:108
  207.3 1.7 fusion.62
  209.1 2.8 reshape.191
  211.9 3.9 reshape.192
  215.8 3.9 reshape.190
  219.6 3.0 fusion.28
  222.7 5.4 fusion.64
  228.0 4.5 fusion.35
  232.5 0.8 copy.47
  233.5 30.4 %all-gather.9.cloned.1.call-done = bf16[512,4096]{1,0:T(8,128)(2,1)} async-done(((bf16[512,512]{1,0:T(8,128)(2,1)}), bf16[512,4096]{1,0:T(8,128)(2,1)}) %all-gather.9.cloned.1.call-update) | async-done | bytes 4194320 | tf_op jit(solution)/shard_map/all_gather | solution.py:135
  263.9 8.9 %convolution_convert_fusion = bf16[1024,4096]{1,0:T(8,128)(2,1)} fusion(bf16[1024,512]{0,1:T(8,128)(2,1)S(1)} %bitcast.81, bf16[512,4096]{1,0:T(8,128)(2,1)} %all-gather.9.cloned.1.call-done), kind=kOutput, calls=%fused_computation.29 | convolution fusion | flops 4299161600 | bytes 13631488 | tf_op jit(solution)/shard_map/dot_general | solution.py:133
  273.0 0.6 copy-done.7
  273.7 5.1 convolution_convert_fusion.2
  278.8 6.7 %psum.36 = bf16[8,512]{1,0:T(8,128)(2,1)S(1)} all-reduce(bf16[8,512]{1,0:T(8,128)(2,1)S(1)} %convolution_convert_fusion.2), channel_id=1, replica_groups=mesh['psg'=8,'mp'=4] {'mp'}, use_global_device_ids=true, to_apply=%region_4.5 | all-reduce | flops 4096 | bytes 16384 | tf_op jit(solution)/shard_map/psum | solution.py:146
  285.7 19.2 %psum.37 = f32[8]{0:T(128)S(1)} all-reduce(f32[8]{0:T(128)S(1)} %multiply_reduce_fusion), channel_id=1, replica_groups=mesh['psg'=8,'mp'=4] {'psg'}, use_global_device_ids=true, to_apply=%region_6.7 | all-reduce | flops 8 | bytes 64 | tf_op jit(solution)/shard_map/psum | solution.py:148
  305.8 33.1 %psum.38 = f32[8,8,64]{2,0,1:T(8,128)S(1)} all-reduce(f32[8,8,64]{2,0,1:T(8,128)S(1)} %copy.49), channel_id=1, replica_groups=mesh['psg'=8,'mp'=4] {'psg'}, use_global_device_ids=true, to_apply=%region_7.8 | all-reduce | flops 4096 | bytes 32768 | tf_op jit(solution)/shard_map/psum | solution.py:150
  339.4 31.5 %all_gather.29 = bf16[8,8,4096]{2,0,1:T(8,128)(2,1)S(1)} all-gather(bf16[8,8,512]{2,0,1:T(8,128)(2,1)S(1)} %fusion.44), channel_id=1, replica_groups=mesh['psg'=8,'mp'=4] {'psg'}, dimensions={2}, use_global_device_ids=true | all-gather | bytes 589824 | tf_op jit(solution)/shard_map/all_gather | solution.py:160
  370.9 53.5 %all-reduce.3.cloned.1.call-done = bf16[1024,4096]{1,0:T(8,128)(2,1)} async-done(((bf16[1024,4096]{1,0:T(8,128)(2,1)}), bf16[1024,4096]{1,0:T(8,128)(2,1)}) %all-reduce.3.cloned.1.call-update) | async-done | bytes 8388624 | tf_op jit(solution)/shard_map/psum | solution.py:138
  424.4 7.8 %fusion.4 = (f32[1024]{0:T(1024)S(1)}, bf16[1024,4096]{1,0:T(8,128)(2,1)S(1)}) fusion(bf16[1024,4096]{1,0:T(8,128)(2,1)} %all-reduce.3.cloned.1.call-done, bf16[1024,4096]{1,0:T(8,128)(2,1)} %param.18), kind=kLoop, calls=%fused_computation.14 | loop fusion | flops 29359104 | bytes 25169920 | tf_op jit(solution)/shard_map/reduce_sum | solution.py:66
  432.2 2.9 fusion.65
  435.4 6.4 %fusion.18 = f32[8,8,4096]{2,1,0:T(8,128)} fusion(bf16[1024,4096]{1,0:T(8,128)(2,1)S(1)} %get-tuple-element.200, f32[4096]{0:T(1024)S(1)} %copy-done.11, f32[1024]{0:T(1024)S(1)} %add_rsqrt_fusion, f32[8,8,1024]{2,1,0:T(8,128)S(1)} %get-tuple-element.209, f32[8,8]{1,0:T(8,128)S(1)} %get-tuple-element.208, pred[8,1024]{1,0:T(8,128)(4,1)S(1)} %broadcast_and_fusion), kind=kOutput, calls=%fused_computation.31 | convolution fusion | flops 3238133760 | bytes 9728256 | tf_op jit(solution)/shard_map/rht,td->rhd/dot_general | solution.py:170
  442.3 31.6 %all-gather.1 = f32[64,8]{1,0:T(8,128)S(1)} all-gather(f32[8,8]{1,0:T(8,128)S(1)} %fusion.46), channel_id=3, replica_groups=mesh['psg'=8,'mp'=4] {'psg'}, dimensions={0}, use_global_device_ids=true | all-gather | bytes 2304 | tf_op jit(solution)/shard_map/all_gather | solution.py:21
  474.0 31.6 %all-gather = f32[64,8]{1,0:T(8,128)S(1)} all-gather(f32[8,8]{1,0:T(8,128)S(1)} %get-tuple-element.208), channel_id=2, replica_groups=mesh['psg'=8,'mp'=4] {'psg'}, dimensions={0}, use_global_device_ids=true | all-gather | bytes 2304 | tf_op jit(solution)/shard_map/all_gather | solution.py:21
  505.6 61.5 %all-gather.11.cloned.1.call-done = f32[64,8,4096]{2,1,0:T(8,128)} async-done(((f32[8,8,4096]{2,1,0:T(8,128)}), f32[64,8,4096]{2,1,0:T(8,128)}) %all-gather.11.cloned.1.call-update) | async-done | bytes 8388624 | tf_op jit(solution)/shard_map/all_gather | solution.py:21
  567.1 1.3 slice.65
  568.4 12.4 %while.19 = (s32[]{:T(128)}, f32[8,8]{1,0:T(8,128)S(1)}, f32[8,8]{1,0:T(8,128)S(1)}, f32[8,8,4096]{2,1,0:T(8,128)S(1)}, f32[8,8,8]{2,1,0:T(8,128)S(1)}, /*index=...) while((s32[]{:T(128)}, f32[8,8]{1,0:T(8,128)S(1)}, ...), condition=%wide.region_12.13_spmd, body=%wide.region_11.12_spmd.sunk | while | flops 786821 | bytes 3148439 | solution.py:27
  568.4 1.8 fusion.82
  570.2 1.7 fusion.82
  572.0 1.7 fusion.82
  573.8 1.7 fusion.82
  575.5 1.7 fusion.82
  577.3 1.7 fusion.82
  579.1 1.7 fusion.82
  581.5 34.2 %psum.39 = f32[8,512]{1,0:T(8,128)S(1)} all-reduce(f32[8,512]{1,0:T(8,128)S(1)} %reshape.177), channel_id=1, replica_groups=mesh['psg'=8,'mp'=4] {'psg'}, use_global_device_ids=true, to_apply=%region_13.14 | all-reduce | flops 4096 | bytes 32768 | tf_op jit(solution)/shard_map/psum | solution.py:180
  615.8 0.9 fusion.66
  616.7 3.1 constant_dynamic-slice_fusion
  619.8 13.8 %reduce-scatter.2.cloned.1.call-done = f32[8,128]{1,0:T(8,128)} async-done(((f32[8,512]{1,0:T(8,128)}), f32[8,128]{1,0:T(8,128)}) %reduce-scatter.2.cloned.1.call-update) | async-done | bytes 4112 | tf_op jit(solution)/shard_map/reduce_scatter | solution.py:186
  633.6 1.3 add_convert_fusion
  (77 shorter events, 3.9 us)
Async XLA Ops:
  7.2 297.7 %copy-start = (bf16[512,512]{1,0:T(8,128)(2,1)S(1)}, bf16[512,512]{1,0:T(8,128)(2,1)}, u32[]{:S(2)}) copy-start(bf16[512,512]{1,0:T(8,128)(2,1)} %param.30) | copy-start | bytes 1572868
  7.2 181.8 %all-gather.7.cloned.1.call-start = ((), (), s32[]{:S(2)}) async-start(), calls=%async_computation.1 | async-start | bytes 14155776 | tf_op jit(solution)/shard_map/all_gather | solution.py:111
  7.9 256.0 %all-gather.9.cloned.1.call-start = ((), (), s32[]{:S(2)}) async-start(), calls=%async_computation.2 | async-start | bytes 4718592 | tf_op jit(solution)/shard_map/all_gather | solution.py:135
  8.7 415.7 %all-reduce.3.cloned.1.call-start = ((), (), s32[]{:S(2)}) async-start(), calls=%async_computation.3 | async-start | bytes 16777216 | tf_op jit(solution)/shard_map/psum | solution.py:138
  12.6 12.1 %copy-start.9 = (s32[4]{0:T(128)S(1)}, s32[4]{0:T(128)}, u32[]{:S(2)}) copy-start(s32[4]{0:T(128)} %param.19) | copy-start | bytes 52
  20.5 168.5 %copy-start.10 = (f32[4096]{0:T(1024)S(1)}, f32[4096]{0:T(1024)}, u32[]{:S(2)}) copy-start(f32[4096]{0:T(1024)} %param.22) | copy-start | bytes 49156
  219.6 3.0 copy-start.3
  222.7 5.4 copy-start.2
  272.8 0.7 copy-start.7
  272.9 32.0 %copy-start.6 = (f32[512]{0:T(512)S(1)}, f32[512]{0:T(512)}, u32[]{:S(2)}) copy-start(f32[512]{0:T(512)} %param.29) | copy-start | bytes 6148
  272.9 32.4 %copy-start.4 = (bf16[2,512,512]{2,1,0:T(8,128)(2,1)S(1)}, bf16[2,512,512]{2,1,0:T(8,128)(2,1)}, u32[]{:S(2)}) copy-start(bf16[2,512,512]{2,1,0:T(8,128)(2,1)} %param.31) | copy-start | bytes 3145732
  272.9 294.2 %all-gather.11.cloned.1.call-start = ((), (), s32[]{:S(2)}) async-start(), calls=%async_computation.5 | async-start | bytes 9437184 | tf_op jit(solution)/shard_map/all_gather | solution.py:21
  273.7 31.9 %copy-start.8 = (f32[4]{0:T(128)S(1)}, f32[4]{0:T(128)}, u32[]{:S(2)}) copy-start(f32[4]{0:T(128)} %param.21) | copy-start | bytes 52
  273.7 65.2 %copy-start.12 = (s32[4]{0:T(128)S(1)}, s32[4]{0:T(128)}, u32[]{:S(2)}) copy-start(s32[4]{0:T(128)} %param.20) | copy-start | bytes 52
  370.9 61.3 %copy-start.11 = (f32[4096]{0:T(1024)S(1)}, f32[4096]{0:T(1024)}, u32[]{:S(2)}) copy-start(f32[4096]{0:T(1024)} %param.26) | copy-start | bytes 49156
  432.2 3.2 copy-start.1
  441.9 191.8 %reduce-scatter.2.cloned.1.call-start = ((), (), s32[]{:S(2)}) async-start(), calls=%async_computation.4 | async-start | bytes 20480 | tf_op jit(solution)/shard_map/reduce_scatter | solution.py:186
  568.4 47.4 %copy-start.5 = (bf16[512,512]{1,0:T(8,128)(2,1)S(1)}, bf16[512,512]{1,0:T(8,128)(2,1)}, u32[]{:S(2)}) copy-start(bf16[512,512]{1,0:T(8,128)(2,1)} %param.32) | copy-start | bytes 1572868
Sparse Core Ops, SparseCore 0:
  10.2 178.8 all-gather.6
  191.1 72.8 all-gather.8
  273.0 151.3 all-reduce.2
  442.0 125.0 all-gather.10
  616.8 16.7 reduce-scatter.1
where the time goes:
time: 642 us; the launch traced here: 641 us
  waiting for transfers between devices  320 us (50%)
  blocking collectives  188 us (29%)
  matrix products  52.2 us (8%)
  local copies, waits for them, and re-layouts  34.7 us (5%)
  other arithmetic  32.4 us (5%)
  between operations  14.1 us (2%)
    all_gather x1, waiting for transfers between devices, shards(): lax.all_gather(enc_qkv, 'psg', axis=1, tiled=True)  159 us
    all_gather x2, blocking collectives, merged(): everything = jax.tree.map(lambda part: lax.all_gather(part, axis), value)  63.2 us
    all_gather x1, waiting for transfers between devices, merged(): everything = jax.tree.map(lambda part: lax.all_gather(part, axis), value)  61.5 us
    psum x1, waiting for transfers between devices, shards(): summed = lax.psum(partial_out, 'mp').astype(jnp.float32)  53.5 us
    psum x1, blocking collectives, shards(): cross_attn = lax.psum(value_terms, 'psg')  34.2 us
    psum x1, blocking collectives, shards(): cquery = lax.psum(jnp.dot(dquery, query_weight, precision=HIGHEST), 'psg')  33.1 us
    all_gather x1, blocking collectives, shards(): lax.all_gather(folded.astype(jnp.bfloat16), 'psg', axis=2, tiled=True)  31.5 us
    all_gather x1, waiting for transfers between devices, shards(): lax.all_gather(enc_output, 'psg', axis=1, tiled=True)  30.4 us
  transfers between devices with their start and end apart: 5, of which 5 were waited for; matrix products, arithmetic and copies ran while one was open for 12% of the time, Pallas kernels for 0%

commit v1 on v0

--- a/solution.py
+++ b/solution.py
@@ -15,6 +15,18 @@
 EPSILON = 1e-06
 MASKED = -1e30
 HIGHEST = lax.Precision.HIGHEST
+
+
+def doubled_up(value, axis, dim):
+    ways, here = (lax.axis_size(axis), lax.axis_index(axis))
+    grown, reach = (value, 1)
+    while reach < ways:
+        theirs = lax.ppermute(grown, axis, [(d, d ^ reach) for d in range(ways)])
+        mine_first = jnp.concatenate([grown, theirs], axis=dim)
+        theirs_first = jnp.concatenate([theirs, grown], axis=dim)
+        grown = jnp.where(here & reach == 0, mine_first, theirs_first)
+        reach = 2 * reach
+    return grown
 
 
 def merged(value, axis, combine):
@@ -106,10 +118,7 @@
     groups_count = lax.axis_size("mp")
     normed = rms_norm(tokens, enc_gain).astype(jnp.bfloat16)
     projected = jnp.einsum(
-        "td,kdc->ktc",
-        normed,
-        lax.all_gather(enc_qkv, "psg", axis=1, tiled=True),
-        preferred_element_type=jnp.float32,
+        "td,kdc->ktc", normed, doubled_up(enc_qkv, "psg", 1), preferred_element_type=jnp.float32
     )
     shaped = projected.astype(jnp.bfloat16).reshape(3, passages_here, SEQ, heads_here, HEAD_DIM)
     bias_table = jnp.dot(

time: 642 us -> 873 us (1.36)
  waiting for transfers between devices: 320 us -> 531 us
  other arithmetic: 32.4 us -> 45.6 us
    ppermute x0 -> x3, waiting for transfers between devices: none -> 402 us  [doubled_up(): theirs = lax.ppermute(grown, axis, [(d, d ^ reach) for d in range(ways)])]
    all_gather x1 -> x0, waiting for transfers between devices: 159 us -> none  [shards(): lax.all_gather(enc_qkv, 'psg', axis=1, tiled=True)]
    all_gather x1, waiting for transfers between devices: 30.4 us -> 0.02 us  [shards(): lax.all_gather(enc_output, 'psg', axis=1, tiled=True)]
    select_n x0 -> x2, other arithmetic: none -> 13.2 us  [doubled_up(): grown = jnp.where(here & reach == 0, mine_first, theirs_first)]
  transfers between devices with their start and end apart: 5 -> 7, of which waited for: 5 -> 6; matrix products, arithmetic and copies ran while one was open for 12% -> 8% of each run, Pallas kernels for 0% -> 0%
where the time goes in v1:
time: 873 us
  waiting for transfers between devices  531 us (61%)
  blocking collectives  191 us (22%)
  matrix products  51.8 us (6%)
  other arithmetic  45.6 us (5%)
  local copies, waits for them, and re-layouts  31.1 us (4%)
  between operations  14.1 us (2%)
    ppermute x3, waiting for transfers between devices, doubled_up(): theirs = lax.ppermute(grown, axis, [(d, d ^ reach) for d in range(ways)])  402 us
    all_gather x2, blocking collectives, merged(): everything = jax.tree.map(lambda part: lax.all_gather(part, axis), value)  63.2 us
    all_gather x1, waiting for transfers between devices, merged(): everything = jax.tree.map(lambda part: lax.all_gather(part, axis), value)  61.5 us
    psum x1, waiting for transfers between devices, shards(): summed = lax.psum(partial_out, 'mp').astype(jnp.float32)  53.4 us
    psum x1, blocking collectives, shards(): cross_attn = lax.psum(value_terms, 'psg')  34.2 us
    psum x1, blocking collectives, shards(): cquery = lax.psum(jnp.dot(dquery, query_weight, precision=HIGHEST), 'psg')  33.2 us
    all_gather x1, blocking collectives, shards(): lax.all_gather(folded.astype(jnp.bfloat16), 'psg', axis=2, tiled=True)  31.5 us
    psum x1, blocking collectives, shards(): squares_dec = lax.psum(jnp.sum(embedded * embedded, axis=1), 'psg')  22.3 us
  transfers between devices with their start and end apart: 7, of which 6 were waited for; matrix products, arithmetic and copies ran while one was open for 8% of the time, Pallas kernels for 0%

profile of v1, /device:TPU:0, one launch (start us, length us, event | category | flops | bytes accessed | tf_op | source)
XLA Modules:
  0.0 872.5 jit_solution(9287941861875749332)
XLA Ops:
  7.2 3.0 collective-permute-start
  10.3 34.6 %collective-permute-done = bf16[3,512,512]{2,1,0:T(8,128)(2,1)S(1)} collective-permute-done((bf16[3,512,512]{2,1,0:T(8,128)(2,1)}, bf16[3,512,512]{2,1,0:T(8,128)(2,1)S(1)}, u32[]{:S(2)}, u32[]{:S(2)}) %collective-permute-start) | collective-permute-done | bytes 1572896 | tf_op jit(solution)/shard_map/ppermute | solution.py:24
  44.9 3.6 maximum_select_fusion.3
  48.4 1.8 collective-permute-start.1
  50.3 67.8 %collective-permute-done.1 = bf16[3,1024,512]{2,1,0:T(8,128)(2,1)} collective-permute-done((bf16[3,1024,512]{2,1,0:T(8,128)(2,1)}, bf16[3,1024,512]{2,1,0:T(8,128)(2,1)}, u32[]{:S(2)}, u32[]{:S(2)}) %collective-permute-start.1) | collective-permute-done | bytes 3145760 | tf_op jit(solution)/shard_map/ppermute | solution.py:24
  118.0 9.6 %maximum_select_fusion.2 = bf16[3,2048,512]{2,1,0:T(8,128)(2,1)} fusion(bf16[3,1024,512]{2,1,0:T(8,128)(2,1)} %collective-permute-done.1, bf16[3,1024,512]{2,1,0:T(8,128)(2,1)} %maximum_select_fusion.3, pred[]{:T(512)S(6)} %eq.41), kind=kLoop, calls=%fused_computation.38 | loop fusion | flops 28311552 | bytes 12582913 | tf_op jit(solution)/shard_map/jit(_where)/select_n | solution.py:27
  127.6 2.6 collective-permute-start.2
  131.2 2.2 slice.61
  133.5 7.9 reshape.172
  141.3 1.8 slice.62
  143.2 2.0 copy.41
  145.2 5.1 fusion.7
  150.3 299.9 %collective-permute-done.2 = bf16[3,2048,512]{2,1,0:T(8,128)(2,1)} collective-permute-done((bf16[3,2048,512]{2,1,0:T(8,128)(2,1)}, bf16[3,2048,512]{2,1,0:T(8,128)(2,1)}, u32[]{:S(2)}, u32[]{:S(2)}) %collective-permute-start.2) | collective-permute-done | bytes 6291488 | tf_op jit(solution)/shard_map/ppermute | solution.py:24
  450.2 21.1 %convert_bitcast_fusion = bf16[3,1024,512]{1,2,0:T(8,128)(2,1)} fusion(bf16[1024,4096]{1,0:T(8,128)(2,1)} %param.18, f32[4096]{0:T(1024)S(1)} %copy-done.12, f32[1024]{0:T(1024)S(1)} %add_rsqrt_fusion.1, bf16[3,2048,512]{2,1,0:T(8,128)(2,1)} %collective-permute-done.2, bf16[3,2048,512]{2,1,0:T(8,128)(2,1)} %maximum_select_fusion.2, pred[]{:T(512)S(6)} %eq.40), kind=kOutput, calls=%fused_computation.46 | convolution fusion | flops 12959875072 | bytes 24137728 | tf_op jit(solution)/shard_map/td,kdc->ktc/dot_general | solution.py:120
  471.3 3.5 fusion.65
  475.6 1.9 squeeze.52
  477.5 2.7 squeeze.50
  480.2 1.3 fusion.44
  481.8 5.3 fusion.67
  487.1 4.2 fusion.35
  491.3 0.8 copy.44
  492.4 9.0 %convolution_convert_fusion = bf16[1024,4096]{1,0:T(8,128)(2,1)} fusion(bf16[1024,512]{0,1:T(8,128)(2,1)S(1)} %bitcast.86, bf16[512,4096]{1,0:T(8,128)(2,1)} %all-gather.6.cloned.1.call-done), kind=kOutput, calls=%fused_computation.36 | convolution fusion | flops 4299161600 | bytes 13631488 | tf_op jit(solution)/shard_map/dot_general | solution.py:142
  502.2 4.6 convolution_convert_fusion.2
  506.8 6.7 psum.36
  513.6 22.3 %psum.37 = f32[8]{0:T(128)S(1)} all-reduce(f32[8]{0:T(128)S(1)} %multiply_reduce_fusion), channel_id=1, replica_groups=mesh['psg'=8,'mp'=4] {'psg'}, use_global_device_ids=true, to_apply=%region_6.7 | all-reduce | flops 8 | bytes 64 | tf_op jit(solution)/shard_map/psum | solution.py:157
  536.9 33.2 %psum.38 = f32[8,8,64]{2,0,1:T(8,128)S(1)} all-reduce(f32[8,8,64]{2,0,1:T(8,128)S(1)} %copy.46), channel_id=1, replica_groups=mesh['psg'=8,'mp'=4] {'psg'}, use_global_device_ids=true, to_apply=%region_7.8 | all-reduce | flops 4096 | bytes 32768 | tf_op jit(solution)/shard_map/psum | solution.py:159
  570.5 31.5 %all_gather.25 = bf16[8,8,4096]{2,0,1:T(8,128)(2,1)S(1)} all-gather(bf16[8,8,512]{2,0,1:T(8,128)(2,1)S(1)} %fusion.42), channel_id=1, replica_groups=mesh['psg'=8,'mp'=4] {'psg'}, dimensions={2}, use_global_device_ids=true | all-gather | bytes 589824 | tf_op jit(solution)/shard_map/all_gather | solution.py:169
  602.1 53.4 %all-reduce.3.cloned.1.call-done = bf16[1024,4096]{1,0:T(8,128)(2,1)} async-done(((bf16[1024,4096]{1,0:T(8,128)(2,1)}), bf16[1024,4096]{1,0:T(8,128)(2,1)}) %all-reduce.3.cloned.1.call-update) | async-done | bytes 8388624 | tf_op jit(solution)/shard_map/psum | solution.py:147
  655.5 7.8 fusion.4
  663.3 2.9 fusion.68
  666.5 6.4 fusion.24
  673.5 31.6 %all-gather.1 = f32[64,8]{1,0:T(8,128)S(1)} all-gather(f32[8,8]{1,0:T(8,128)S(1)} %fusion.48), channel_id=3, replica_groups=mesh['psg'=8,'mp'=4] {'psg'}, dimensions={0}, use_global_device_ids=true | all-gather | bytes 2304 | tf_op jit(solution)/shard_map/all_gather | solution.py:33
  705.1 31.6 %all-gather = f32[64,8]{1,0:T(8,128)S(1)} all-gather(f32[8,8]{1,0:T(8,128)S(1)} %get-tuple-element.208), channel_id=2, replica_groups=mesh['psg'=8,'mp'=4] {'psg'}, dimensions={0}, use_global_device_ids=true | all-gather | bytes 2304 | tf_op jit(solution)/shard_map/all_gather | solution.py:33
  736.7 61.5 %all-gather.8.cloned.1.call-done = f32[64,8,4096]{2,1,0:T(8,128)} async-done(((f32[8,8,4096]{2,1,0:T(8,128)}), f32[64,8,4096]{2,1,0:T(8,128)}) %all-gather.8.cloned.1.call-update) | async-done | bytes 8388624 | tf_op jit(solution)/shard_map/all_gather | solution.py:33
  798.2 1.3 slice.65
  799.5 12.4 %while.19 = (s32[]{:T(128)}, f32[8,8]{1,0:T(8,128)S(1)}, f32[8,8]{1,0:T(8,128)S(1)}, f32[8,8,4096]{2,1,0:T(8,128)S(1)}, f32[8,8,8]{2,1,0:T(8,128)S(1)}, /*index=...) while((s32[]{:T(128)}, f32[8,8]{1,0:T(8,128)S(1)}, ...), condition=%wide.region_12.13_spmd, body=%wide.region_11.12_spmd.sunk | while | flops 786821 | bytes 3148439 | solution.py:39
  799.5 1.8 fusion.84
  801.4 1.7 fusion.84
  803.1 1.7 fusion.84
  804.9 1.7 fusion.84
  806.6 1.7 fusion.84
  808.4 1.7 fusion.84
  810.2 1.7 fusion.84
  812.6 34.2 %psum.39 = f32[8,512]{1,0:T(8,128)S(1)} all-reduce(f32[8,512]{1,0:T(8,128)S(1)} %reshape.177), channel_id=1, replica_groups=mesh['psg'=8,'mp'=4] {'psg'}, use_global_device_ids=true, to_apply=%region_13.14 | all-reduce | flops 4096 | bytes 32768 | tf_op jit(solution)/shard_map/psum | solution.py:189
  846.9 0.9 fusion.69
  847.8 3.1 constant_dynamic-slice_fusion
  850.9 13.8 %reduce-scatter.2.cloned.1.call-done = f32[8,128]{1,0:T(8,128)} async-done(((f32[8,512]{1,0:T(8,128)}), f32[8,128]{1,0:T(8,128)}) %reduce-scatter.2.cloned.1.call-update) | async-done | bytes 4112 | tf_op jit(solution)/shard_map/reduce_scatter | solution.py:195
  864.7 1.3 add_convert_fusion
  (86 shorter events, 6.3 us)
Async XLA Ops:
  7.2 528.8 %copy-start = (bf16[512,512]{1,0:T(8,128)(2,1)S(1)}, bf16[512,512]{1,0:T(8,128)(2,1)}, u32[]{:S(2)}) copy-start(bf16[512,512]{1,0:T(8,128)(2,1)} %param.30) | copy-start | bytes 1572868
  7.2 485.2 %all-gather.6.cloned.1.call-start = ((), (), s32[]{:S(2)}) async-start(), calls=%async_computation.1 | async-start | bytes 4718592 | tf_op jit(solution)/shard_map/all_gather | solution.py:144
  7.2 37.6 %collective-permute-start = (bf16[3,512,512]{2,1,0:T(8,128)(2,1)}, bf16[3,512,512]{2,1,0:T(8,128)(2,1)S(1)}, u32[]{:S(2)}, u32[]{:S(2)}) collective-permute-start(bf16[3,512,512]{2,1,0:T(8,128)(2,1)} %param.23), channel_id=1, source_target_pairs={{0,4},{4,0},{8,12},{12,8},{16,20},{20,16},{24,28},{28,24},{1,5},{5... | collective-permute-start | bytes 4718600 | tf_op jit(solution)/shard_map/ppermute | solution.py:24
  10.3 120.0 %copy-start.6 = (f32[32,511]{1,0:T(8,128)S(1)}, f32[32,511]{1,0:T(8,128)}, u32[]{:S(2)}) copy-start(f32[32,511]{1,0:T(8,128)} %constant.93.clone) | copy-start | bytes 196228
  10.3 120.0 %copy-start.7 = (f32[8,32]{1,0:T(8,128)S(1)}, f32[8,32]{1,0:T(8,128)}, u32[]{:S(2)}) copy-start(f32[8,32]{1,0:T(8,128)} %param.24) | copy-start | bytes 3076
  10.3 120.3 %copy-start.11 = (s32[4]{0:T(128)S(1)}, s32[4]{0:T(128)}, u32[]{:S(2)}) copy-start(s32[4]{0:T(128)} %param.19) | copy-start | bytes 52
  48.4 69.6 %collective-permute-start.1 = (bf16[3,1024,512]{2,1,0:T(8,128)(2,1)}, bf16[3,1024,512]{2,1,0:T(8,128)(2,1)}, u32[]{:S(2)}, u32[]{:S(2)}) collective-permute-start(bf16[3,1024,512]{2,1,0:T(8,128)(2,1)} %maximum_select_fusion.3), channel_id=1, source_target_pairs={{0,8},{4,12},{8,0},{12,4},{16,24},{20,28},{24,16},{28,20},{1,9},{5... | collective-permute-start | bytes 9437192 | tf_op jit(solution)/shard_map/ppermute | solution.py:24
  127.6 322.5 %collective-permute-start.2 = (bf16[3,2048,512]{2,1,0:T(8,128)(2,1)}, bf16[3,2048,512]{2,1,0:T(8,128)(2,1)}, u32[]{:S(2)}, u32[]{:S(2)}) collective-permute-start(bf16[3,2048,512]{2,1,0:T(8,128)(2,1)} %maximum_select_fusion.2), channel_id=1, source_target_pairs={{0,16},{4,20},{8,24},{12,28},{16,0},{20,4},{24,8},{28,12},{1,17},{... | collective-permute-start | bytes 18874376 | tf_op jit(solution)/shard_map/ppermute | solution.py:24
  130.2 525.2 %all-reduce.3.cloned.1.call-start = ((), (), s32[]{:S(2)}) async-start(), calls=%async_computation.2 | async-start | bytes 16777216 | tf_op jit(solution)/shard_map/psum | solution.py:147
  141.3 308.9 %copy-start.12 = (f32[4096]{0:T(1024)S(1)}, f32[4096]{0:T(1024)}, u32[]{:S(2)}) copy-start(f32[4096]{0:T(1024)} %param.22) | copy-start | bytes 49156
  480.2 1.6 copy-start.2
  481.8 5.3 copy-start.4
  501.4 0.7 copy-start.9
  501.4 34.5 %copy-start.8 = (f32[512]{0:T(512)S(1)}, f32[512]{0:T(512)}, u32[]{:S(2)}) copy-start(f32[512]{0:T(512)} %param.29) | copy-start | bytes 6148
  501.4 35.0 %copy-start.3 = (bf16[2,512,512]{2,1,0:T(8,128)(2,1)S(1)}, bf16[2,512,512]{2,1,0:T(8,128)(2,1)}, u32[]{:S(2)}) copy-start(bf16[2,512,512]{2,1,0:T(8,128)(2,1)} %param.31) | copy-start | bytes 3145732
  501.4 296.8 %all-gather.8.cloned.1.call-start = ((), (), s32[]{:S(2)}) async-start(), calls=%async_computation.4 | async-start | bytes 9437184 | tf_op jit(solution)/shard_map/all_gather | solution.py:33
  502.2 34.5 %copy-start.10 = (f32[4]{0:T(128)S(1)}, f32[4]{0:T(128)}, u32[]{:S(2)}) copy-start(f32[4]{0:T(128)} %param.21) | copy-start | bytes 52
  502.2 67.8 %copy-start.14 = (s32[4]{0:T(128)S(1)}, s32[4]{0:T(128)}, u32[]{:S(2)}) copy-start(s32[4]{0:T(128)} %param.20) | copy-start | bytes 52
  602.0 61.3 %copy-start.13 = (f32[4096]{0:T(1024)S(1)}, f32[4096]{0:T(1024)}, u32[]{:S(2)}) copy-start(f32[4096]{0:T(1024)} %param.26) | copy-start | bytes 49156
  663.3 3.2 copy-start.1
  673.0 191.8 %reduce-scatter.2.cloned.1.call-start = ((), (), s32[]{:S(2)}) async-start(), calls=%async_computation.3 | async-start | bytes 20480 | tf_op jit(solution)/shard_map/reduce_scatter | solution.py:195
  799.5 47.4 %copy-start.5 = (bf16[512,512]{1,0:T(8,128)(2,1)S(1)}, bf16[512,512]{1,0:T(8,128)(2,1)}, u32[]{:S(2)}) copy-start(bf16[512,512]{1,0:T(8,128)(2,1)} %param.32) | copy-start | bytes 1572868
Sparse Core Ops, SparseCore 0:
  130.3 219.9 all-gather.5
  501.5 153.9 all-reduce.2
  673.1 125.0 all-gather.7
  847.9 16.7 reduce-scatter.1
